TPU v7x, 32 devices: a whole 2x2x4 slice. The times are simulated.
32 devices in a mesh: seq: 4 (over z), expert: 8 (over y, x, core).
Axes of the slice: x: 2, y: 2, z: 4, core: 2. Of those that a mesh axis runs over, the one named last changes fastest.
Arguments:
- residual: bfloat16 [8, 512, 2048], P('expert', 'seq'), may hold values from -6 to 6
- queries: bfloat16 [8, 512, 2048], P('expert', 'seq'), may hold values from -400 to 400
- key_input: bfloat16 [8, 512, 512], P('expert', 'seq'), may hold values from -4 to 4
- value_input: bfloat16 [8, 512, 512], P('expert', 'seq'), may hold values from -6 to 6
- routes: int32 [8, 512, 6], P('expert', 'seq'), may hold values from 0 to 15, all different within a row; in each aligned block of 128 rows (0 to 127, 128 to 255, ..., all dimensions but the last counted through in order) at most 60 rows name the same one
- mix_weights: float32 [8, 512, 6], P('expert', 'seq'), may hold values from 0.1 to 1
- gate_weight: bfloat16 [16, 2048, 704], P('expert'), may hold values from -0.125 to 0.125
- up_weight: bfloat16 [16, 2048, 704], P('expert'), may hold values from -0.125 to 0.125
- down_weight: bfloat16 [16, 704, 2048], P('expert'), may hold values from -0.21875 to 0.21875
- grad_out: bfloat16 [8, 512, 2048], P('expert', 'seq'), may hold values from -6 to 6
Outputs:
- layer_out: bfloat16 [8, 512, 2048], P('expert', 'seq')
- residual_grad: bfloat16 [8, 512, 2048], P('expert', 'seq')
- query_grad: bfloat16 [8, 512, 2048], P('expert', 'seq')
- key_grad: bfloat16 [8, 512, 512], P('expert', 'seq')
- value_grad: bfloat16 [8, 512, 512], P('expert', 'seq')
- mix_grad: float32 [8, 512, 6], P('expert', 'seq')
- gate_weight_grad: bfloat16 [16, 2048, 704], P('expert', 'seq')
- up_weight_grad: bfloat16 [16, 2048, 704], P('expert', 'seq')
- down_weight_grad: bfloat16 [16, 704, 2048], P('expert', None, 'seq')
Inputs may be any that keep to these rules, and one draw needn't show every extreme that they name: `routes`: each row names 6 different experts. Among the rows of one device no expert is named by more than 60 rows, and in every draw some expert is named by exactly 60 rows of some device.
All inputs are finite; a program needn't handle non-finite values.
Results may differ from a plain program's by a relative error of at most 0.04.
Values may be sent and summed in bfloat16 or wider, within the bound.
A program may use at most 192 MiB of HBM per device.

v0:
```python
import math

import jax
import jax.numpy as jnp
from jax import lax
from jax.sharding import PartitionSpec as P

DH = 128


neg_big = -1e30
norm_eps = 1e-06


def fold_keys(key_rows, value_rows, combine, initial):
    return combine(
        initial,
        (
            lax.all_gather(key_rows, "seq", axis=0, tiled=True),
            lax.all_gather(value_rows, "seq", axis=0, tiled=True),
        ),
        jnp.int32(0),
    )


def collect_rows(results):
    return lax.all_to_all(results, "expert", split_axis=1, concat_axis=1, tiled=True)


def silu_grads(act_grad, gate_pre, up_pre):
    sigmoid = jax.nn.sigmoid(gate_pre)
    gate_grad = (act_grad * up_pre * sigmoid * (1.0 + gate_pre * (1.0 - sigmoid))).astype(
        jnp.bfloat16
    )
    up_grad = (act_grad * gate_pre * sigmoid).astype(jnp.bfloat16)
    return (gate_grad, up_grad)


def dense_forward(expert_rows, gate_weight, up_weight, down_weight):
    gate_pre = jnp.einsum(
        "erd,edf->erf", expert_rows, gate_weight, preferred_element_type=jnp.float32
    )
    up_pre = jnp.einsum("erd,edf->erf", expert_rows, up_weight, preferred_element_type=jnp.float32)
    activation = (jax.nn.silu(gate_pre) * up_pre).astype(jnp.bfloat16)
    results = jnp.einsum(
        "erf,efd->erd", activation, down_weight, preferred_element_type=jnp.float32
    ).astype(jnp.bfloat16)
    return (results, (gate_pre, up_pre, activation))


def dense_backward(expert_rows, grad_rows, kept_values, gate_weight, up_weight, down_weight):
    gate_pre, up_pre, activation = kept_values
    act_grad = jnp.einsum(
        "erd,efd->erf", grad_rows, down_weight, preferred_element_type=jnp.float32
    )
    gate_grad, up_grad = silu_grads(act_grad, gate_pre, up_pre)
    input_grad = jnp.einsum(
        "erf,edf->erd", gate_grad, gate_weight, preferred_element_type=jnp.float32
    )
    input_grad = (
        input_grad
        + jnp.einsum("erf,edf->erd", up_grad, up_weight, preferred_element_type=jnp.float32)
    ).astype(jnp.bfloat16)
    gate_sum = jnp.einsum(
        "erd,erf->edf", expert_rows, gate_grad, preferred_element_type=jnp.float32
    )
    up_sum = jnp.einsum("erd,erf->edf", expert_rows, up_grad, preferred_element_type=jnp.float32)
    down_sum = jnp.einsum("erf,erd->efd", activation, grad_rows, preferred_element_type=jnp.float32)
    return (input_grad, (gate_sum, up_sum, down_sum))


def expert_forward(expert_rows, gate_weight, up_weight, down_weight):
    results, kept_values = dense_forward(expert_rows, gate_weight, up_weight, down_weight)
    return (results, (None, kept_values))


def expert_backward(expert_rows, grad_rows, kept_state, gate_weight, up_weight, down_weight):
    tile_plan, kept_values = kept_state
    return dense_backward(expert_rows, grad_rows, kept_values, gate_weight, up_weight, down_weight)


def on_device(
    residual,
    queries,
    key_input,
    value_input,
    routes,
    mix_weights,
    gate_weight,
    up_weight,
    down_weight,
    grad_out,
):
    tokens = residual.shape[1]
    width = residual.shape[2]
    kv_width = key_input.shape[2]
    kv_heads = kv_width // DH
    q_heads = queries.shape[2] // DH
    group_size = q_heads // kv_heads
    expert_local = gate_weight.shape[0]
    expert_ranks = lax.axis_size("expert")
    experts_all = expert_local * expert_ranks
    top_count = routes.shape[2]
    capacity = tokens * top_count * 5 // (4 * experts_all)
    total_slots = experts_all * capacity
    inv_scale = 1.0 / math.sqrt(DH)
    query_rows = queries.reshape(tokens, kv_heads, group_size, DH)
    key_rows = key_input.reshape(tokens, kv_width)
    value_rows = value_input.reshape(tokens, kv_width)
    row_pos = lax.axis_index("seq") * tokens + jnp.arange(tokens, dtype=jnp.int32)

    def block_scores(key_part):
        piece_rows = key_part.shape[0]
        key_heads = key_part.reshape(piece_rows, kv_heads, DH)
        scores = (
            jnp.einsum("tkgd,jkd->tkgj", query_rows, key_heads, preferred_element_type=jnp.float32)
            * inv_scale
        )
        key_pos = jnp.arange(piece_rows, dtype=jnp.int32)
        visible = (key_pos[None, :] <= row_pos[:, None])[:, None, None, :]
        return (key_heads, scores, visible)

    def attend(carried, pieces, offset):
        run_max, run_sum, accumulated = carried
        key_part, value_part = pieces
        key_heads, scores, visible = block_scores(key_part)
        masked = jnp.where(visible, scores, neg_big)
        new_max = jnp.maximum(run_max, jnp.max(masked, axis=3))
        weights = jnp.where(visible, jnp.exp(masked - new_max[..., None]), 0.0)
        value_heads = value_part.reshape(key_part.shape[0], kv_heads, DH)
        update = jnp.einsum(
            "tkgj,jkd->tkgd",
            weights.astype(jnp.bfloat16),
            value_heads,
            preferred_element_type=jnp.float32,
        )
        return (new_max, jnp.sum(weights, axis=3), update)

    state_shape = (tokens, kv_heads, group_size)
    initial = (
        jnp.full(state_shape, neg_big, jnp.float32),
        jnp.zeros(state_shape, jnp.float32),
        jnp.zeros(state_shape + (DH,), jnp.float32),
    )
    run_max, run_sum, accumulated = fold_keys(key_rows, value_rows, attend, initial)
    attention = (accumulated / run_sum[..., None]).astype(jnp.bfloat16)
    log_total = run_max + jnp.log(run_sum)
    hidden_state = residual.reshape(tokens, width).astype(jnp.float32) + attention.reshape(
        tokens, width
    ).astype(jnp.float32)
    inv_rms = lax.rsqrt(jnp.mean(hidden_state * hidden_state, axis=1, keepdims=True) + norm_eps)
    normed = hidden_state * inv_rms
    normed_bf = normed.astype(jnp.bfloat16)
    picked_experts = routes.reshape(tokens, top_count)
    expert_ids = jnp.arange(experts_all, dtype=jnp.int32)
    onehot = (picked_experts[:, :, None] == expert_ids[None, None, :]).astype(jnp.int32)
    per_token = jnp.sum(onehot, axis=1)
    earlier = jnp.cumsum(per_token, axis=0) - per_token
    slot_rank = jnp.sum(onehot * earlier[:, None, :], axis=2)
    owner_rank = picked_experts // expert_local
    local_id = picked_experts % expert_local
    slot_index = ((local_id * expert_ranks + owner_rank) * capacity + slot_rank).reshape(-1)
    pair_ids = jnp.arange(tokens * top_count, dtype=jnp.int32)
    slot_pair = jnp.zeros((total_slots,), jnp.int32).at[slot_index].set(pair_ids)
    slot_live = jnp.zeros((total_slots,), jnp.bool_).at[slot_index].set(True)
    slot_token = slot_pair // top_count
    block_shape = (expert_local, expert_ranks, capacity, width)
    zero_bf = jnp.zeros((), jnp.bfloat16)
    outgoing = jnp.where(
        slot_live[:, None], jnp.take(normed_bf, slot_token, axis=0), zero_bf
    ).reshape(block_shape)
    arrived = lax.all_to_all(outgoing, "expert", split_axis=1, concat_axis=1, tiled=True)
    expert_rows = arrived.reshape(expert_local, expert_ranks * capacity, width)
    results, kept_state = expert_forward(expert_rows, gate_weight, up_weight, down_weight)
    returned = collect_rows(results.reshape(block_shape)).reshape(total_slots, width)
    pair_out = jnp.take(returned, slot_index, axis=0).reshape(tokens, top_count, width)
    mix_rows = mix_weights.reshape(tokens, top_count)
    combined = hidden_state + jnp.sum(mix_rows[:, :, None] * pair_out.astype(jnp.float32), axis=1)
    layer_out = combined.astype(jnp.bfloat16)
    grad_rows = grad_out.reshape(tokens, width)
    mix_grad = jnp.einsum("td,tcd->tc", grad_rows, pair_out, preferred_element_type=jnp.float32)
    pair_grad = (
        (mix_rows[:, :, None] * grad_rows.astype(jnp.float32)[:, None, :])
        .astype(jnp.bfloat16)
        .reshape(tokens * top_count, width)
    )
    outgoing_grad = jnp.where(
        slot_live[:, None], jnp.take(pair_grad, slot_pair, axis=0), zero_bf
    ).reshape(block_shape)
    grads_arrived = lax.all_to_all(outgoing_grad, "expert", split_axis=1, concat_axis=1, tiled=True)
    grads_arrived = grads_arrived.reshape(expert_local, expert_ranks * capacity, width)
    input_grad, weight_sums = expert_backward(
        expert_rows, grads_arrived, kept_state, gate_weight, up_weight, down_weight
    )
    input_back = collect_rows(input_grad.reshape(block_shape)).reshape(total_slots, width)
    normed_grad = jnp.sum(
        jnp.take(input_back, slot_index, axis=0)
        .reshape(tokens, top_count, width)
        .astype(jnp.float32),
        axis=1,
    )
    dot_mean = jnp.mean(normed_grad * normed, axis=1, keepdims=True)
    hidden_grad = grad_rows.astype(jnp.float32) + inv_rms * (normed_grad - normed * dot_mean)
    residual_grad = hidden_grad.astype(jnp.bfloat16)
    gate_sum, up_sum, down_sum = weight_sums
    gate_share, up_share, down_share = (
        lax.psum_scatter(
            gate_sum.astype(jnp.bfloat16), "seq", scatter_dimension=1, tiled=True
        ).astype(jnp.float32),
        lax.psum_scatter(
            up_sum.astype(jnp.bfloat16), "seq", scatter_dimension=1, tiled=True
        ).astype(jnp.float32),
        lax.psum_scatter(
            down_sum.astype(jnp.bfloat16), "seq", scatter_dimension=2, tiled=True
        ).astype(jnp.float32),
    )
    out_grad_heads = residual_grad.reshape(tokens, kv_heads, group_size, DH)
    row_delta = jnp.einsum(
        "tkgd,tkgd->tkg", out_grad_heads, attention, preferred_element_type=jnp.float32
    )
    full_len = tokens * lax.axis_size("seq")

    def attend_back(carried, pieces, offset):
        key_part, value_part = pieces
        piece_rows = key_part.shape[0]
        key_heads, scores, visible = block_scores(key_part)
        probabilities = jnp.where(visible, jnp.exp(scores - log_total[..., None]), 0.0)
        value_heads = value_part.reshape(piece_rows, kv_heads, DH)
        prob_grad = jnp.einsum(
            "tkgd,jkd->tkgj", out_grad_heads, value_heads, preferred_element_type=jnp.float32
        )
        score_grad = (probabilities * (prob_grad - row_delta[..., None])).astype(jnp.bfloat16)
        query_acc = (
            jnp.einsum("tkgj,jkd->tkgd", score_grad, key_heads, preferred_element_type=jnp.float32)
            * inv_scale
        )
        key_piece = (
            jnp.einsum("tkgj,tkgd->jkd", score_grad, query_rows, preferred_element_type=jnp.float32)
            * inv_scale
        )
        value_piece = jnp.einsum(
            "tkgj,tkgd->jkd",
            probabilities.astype(jnp.bfloat16),
            out_grad_heads,
            preferred_element_type=jnp.float32,
        )
        return (query_acc, key_piece, value_piece)

    initial_back = (
        jnp.zeros(state_shape + (DH,), jnp.float32),
        jnp.zeros((full_len, kv_heads, DH), jnp.float32),
        jnp.zeros((full_len, kv_heads, DH), jnp.float32),
    )
    query_acc, key_acc, value_acc = fold_keys(key_rows, value_rows, attend_back, initial_back)
    key_share, value_share = (
        lax.psum_scatter(
            key_acc.reshape(full_len, kv_width).astype(jnp.bfloat16),
            "seq",
            scatter_dimension=0,
            tiled=True,
        ).astype(jnp.float32),
        lax.psum_scatter(
            value_acc.reshape(full_len, kv_width).astype(jnp.bfloat16),
            "seq",
            scatter_dimension=0,
            tiled=True,
        ).astype(jnp.float32),
    )
    return (
        layer_out.reshape(1, tokens, width),
        residual_grad.reshape(1, tokens, width),
        query_acc.reshape(1, tokens, q_heads * DH).astype(jnp.bfloat16),
        key_share.astype(jnp.bfloat16).reshape(1, tokens, kv_width),
        value_share.astype(jnp.bfloat16).reshape(1, tokens, kv_width),
        mix_grad.reshape(1, tokens, top_count),
        gate_share.astype(jnp.bfloat16),
        up_share.astype(jnp.bfloat16),
        down_share.astype(jnp.bfloat16),
    )


def solution(mesh):
    placed = (
        P("expert", "seq", None),
        P("expert", "seq", None),
        P("expert", "seq", None),
        P("expert", "seq", None),
        P("expert", "seq", None),
        P("expert", "seq", None),
        P("expert", None, None),
        P("expert", None, None),
        P("expert", None, None),
        P("expert", "seq", None),
    )
    return jax.shard_map(
        on_device,
        mesh=mesh,
        in_specs=placed,
        out_specs=(
            P("expert", "seq", None),
            P("expert", "seq", None),
            P("expert", "seq", None),
            P("expert", "seq", None),
            P("expert", "seq", None),
            P("expert", "seq", None),
            P("expert", "seq", None),
            P("expert", "seq", None),
            P("expert", None, "seq"),
        ),
        check_vma=False,
    )
```

profile of v0, /device:TPU:0, one launch (start us, length us, event | category | flops | bytes accessed | tf_op | source)
XLA Modules:
  0.0 759.4 jit_solution(6643244030811002745)
XLA Ops:
  9.6 3.4 scatter_custom_fusion.1
  14.0 3.4 scatter_custom_fusion
  18.8 16.7 %all-gather = bf16[1,512,512]{1,2,0:T(8,128)(2,1)S(1)} all-gather(bf16[1,128,512]{1,2,0:T(8,128)(2,1)S(1)} %copy.114), channel_id=2, replica_groups=mesh['seq'=4,'expert'=8] {'seq'}, dimensions={1}, use_global_device_ids=true | all-gather | bytes 655360 | tf_op jit(solution)/shard_map/all_gather | solution.py:19
  37.0 15.9 %all-gather.1 = bf16[1,512,512]{2,1,0:T(8,128)(2,1)S(1)} all-gather(bf16[1,128,512]{2,1,0:T(8,128)(2,1)} %param.15), channel_id=3, replica_groups=mesh['seq'=4,'expert'=8] {'seq'}, dimensions={1}, use_global_device_ids=true | all-gather | bytes 655360 | tf_op jit(solution)/shard_map/all_gather | solution.py:20
  58.8 5.9 gather_fusion
  64.7 4.9 gather.16
  69.6 5.6 mul.196
  75.3 8.2 %mul.197 = f32[768,2048]{1,0:T(8,128)} reshape(f32[128,6,2048]{2,1,0:T(8,128)} %mul.196) | data formatting | bytes 12582912 | tf_op jit(solution)/shard_map/mul | solution.py:183
  86.7 5.9 gather_fusion.1
  92.6 4.9 gather.18
  97.5 5.3 select_select_fusion
  102.8 6.0 copy.129
  108.8 4.9 all-to-all-start
  113.8 8.1 %copy.135 = bf16[2,8,60,2048]{3,0,2,1:T(2,128)(2,1)} copy(bf16[2,8,60,2048]{3,2,1,0:T(8,128)(2,1)} %get-tuple-element.58) | data formatting | bytes 7864320 | tf_op jit(solution)/shard_map/jit(_where)/select_n | solution.py:187
  121.9 38.2 %all-to-all-done = bf16[2,8,60,2048]{3,0,2,1:T(2,128)(2,1)} async-done(((bf16[2,8,60,2048]{3,0,2,1:T(2,128)(2,1)}), bf16[2,8,60,2048]{3,0,2,1:T(2,128)(2,1)}, u32[]{:S(2)}, u32[]{:S(2)}) %all-to-all-start) | async-done | bytes 3932192 | tf_op jit(solution)/shard_map/all_to_all | solution.py:172
  160.1 4.7 all-to-all-start.2
  164.8 9.0 %fusion.13 = f32[2,480,704]{1,2,0:T(8,128)} fusion(bf16[2,2048,704]{1,2,0:T(8,128)(2,1)} %param.19, bf16[2,480,2048]{2,0,1:T(2,128)(2,1)} %bitcast.11), kind=kOutput, calls=%fused_computation.38 | convolution fusion | flops 2768240640 | bytes 12402688 | tf_op jit(solution)/shard_map/erd,edf->erf/dot_general | solution.py:43
  173.8 7.0 fusion.15
  180.8 30.3 %all-to-all-done.2 = bf16[2,8,60,2048]{3,0,2,1:T(2,128)(2,1)} async-done(((bf16[2,8,60,2048]{3,0,2,1:T(2,128)(2,1)}), bf16[2,8,60,2048]{3,0,2,1:T(2,128)(2,1)}, u32[]{:S(2)}, u32[]{:S(2)}) %all-to-all-start.2) | async-done | bytes 3932192 | tf_op jit(solution)/shard_map/all_to_all | solution.py:190
  211.0 10.0 %multiply_convert_fusion.1 = (bf16[2,480,704]{1,2,0:T(8,128)(2,1)S(1)}, bf16[2,480,704]{1,2,0:T(8,128)(2,1)S(1)}, bf16[2,480,704]{1,2,0:T(8,128)(2,1)S(1)}) fusion(f32[2,480,704]{1,2,0:T(8,128)} %fusion.15, f32[2,480,704]{1,2,0:T(8,128)} %fusion.13, bf16[2,704,2048]{2,1,0:T(8,128)(2,1)} %param.20, bf16[2,480,2048]{2,0,1:T(2,128)(2,1)} %bitcast.15), kind=kOutput, calls=%fused_computation.32 | convolution fusion | flops 2779054080 | bytes 19161088 | tf_op jit(solution)/shard_map/erd,efd->erf/dot_general | solution.py:53
  221.1 7.9 %convolution_convert_fusion.3 = bf16[2,480,2048]{2,1,0:T(8,128)(2,1)S(1)} fusion(bf16[2,480,704]{1,2,0:T(8,128)(2,1)S(1)} %get-tuple-element.54, bf16[2,704,2048]{2,1,0:T(8,128)(2,1)} %param.20), kind=kOutput, calls=%fused_computation.23 | convolution fusion | flops 2770206720 | bytes 11051008 | tf_op jit(solution)/shard_map/erf,efd->erd/dot_general | solution.py:45
  229.0 5.9 copy.132
  234.9 4.5 all-to-all-start.1
  239.4 5.5 fusion.71
  244.9 6.5 add_convert_fusion
  251.5 6.0 copy.137
  257.5 28.3 %all-to-all-done.1 = bf16[2,8,60,2048]{3,0,2,1:T(2,128)(2,1)} async-done(((bf16[2,8,60,2048]{3,0,2,1:T(2,128)(2,1)}), bf16[2,8,60,2048]{3,0,2,1:T(2,128)(2,1)}, u32[]{:S(2)}, u32[]{:S(2)}) %all-to-all-start.1) | async-done | bytes 3932192 | tf_op jit(solution)/shard_map/all_to_all | solution.py:27
  285.7 4.7 all-to-all-start.3
  293.2 5.9 copy.133
  299.1 5.3 reshape.398
  304.4 32.3 %all-to-all-done.3 = bf16[2,8,60,2048]{3,0,2,1:T(2,128)(2,1)} async-done(((bf16[2,8,60,2048]{3,0,2,1:T(2,128)(2,1)}), bf16[2,8,60,2048]{3,0,2,1:T(2,128)(2,1)}, u32[]{:S(2)}, u32[]{:S(2)}) %all-to-all-start.3) | async-done | bytes 3932192 | tf_op jit(solution)/shard_map/all_to_all | solution.py:27
  336.7 5.9 copy.138
  342.6 4.9 reshape.404
  347.4 9.7 %gather_fusion.2 = bf16[768,2048]{1,0:T(8,128)(2,1)} fusion(bf16[960,2048]{1,0:T(8,128)(2,1)} %reshape.398, s32[1024]{0:T(1024)S(1)} %pad_clamp_fusion.1), kind=kCustom, calls=%fused_computation.clone | custom fusion | bytes 6294528 | tf_op jit(solution)/shard_map/jit(_take)/gather | solution.py:176
  357.2 9.8 %gather_fusion.3 = bf16[768,2048]{1,0:T(8,128)(2,1)} fusion(bf16[960,2048]{1,0:T(8,128)(2,1)} %reshape.404, s32[1024]{0:T(1024)S(1)} %pad_clamp_fusion.1), kind=kCustom, calls=%fused_computation.1.clone | custom fusion | bytes 6294528 | tf_op jit(solution)/shard_map/jit(_take)/gather | solution.py:197
  366.9 7.2 select_convert_fusion
  374.1 8.0 %reshape.411 = f32[128,6,2048]{2,1,0:T(8,128)} reshape(f32[768,2048]{1,0:T(8,128)} %get-tuple-element.60) | data formatting | bytes 12582912 | tf_op jit(solution)/shard_map/convert_element_type | solution.py:199
  382.1 6.1 reduce_sum.81
  394.1 3.9 fusion.1
  401.2 8.5 %convolution_convert_fusion.2 = bf16[2,704,2048]{2,1,0:T(8,128)(2,1)} fusion(bf16[2,480,704]{1,2,0:T(8,128)(2,1)} %copy-done.22, bf16[2,480,2048]{2,0,1:T(2,128)(2,1)} %bitcast.15), kind=kOutput, calls=%fused_computation.11 | convolution fusion | flops 2771124224 | bytes 11051008 | tf_op jit(solution)/shard_map/erf,erd->efd/dot_general | solution.py:68
  409.8 8.5 %convolution_convert_fusion = bf16[2,2048,704]{1,2,0:T(8,128)(2,1)} fusion(bf16[2,480,704]{1,2,0:T(8,128)(2,1)} %copy-done.20, bf16[2,480,2048]{2,0,1:T(2,128)(2,1)} %bitcast.11), kind=kOutput, calls=%fused_computation.9 | convolution fusion | flops 2771124224 | bytes 11051008 | tf_op jit(solution)/shard_map/erd,erf->edf/dot_general | solution.py:67
  418.5 8.6 %convolution_convert_fusion.1 = bf16[2,2048,704]{1,2,0:T(8,128)(2,1)} fusion(bf16[2,480,704]{1,2,0:T(8,128)(2,1)} %copy-done.21, bf16[2,480,2048]{2,0,1:T(2,128)(2,1)} %bitcast.11), kind=kOutput, calls=%fused_computation.10 | convolution fusion | flops 2771124224 | bytes 11051008 | tf_op jit(solution)/shard_map/erd,erf->edf/dot_general | solution.py:64
  433.0 6.3 reshape.400
  439.2 5.1 fusion.43
  445.0 6.2 multiply_reduce_fusion
  452.6 88.9 %reduce-scatter.14.cloned.1.call-done = bf16[2,704,512]{2,1,0:T(8,128)(2,1)} async-done(((bf16[2,704,2048]{2,1,0:T(8,128)(2,1)}), bf16[2,704,512]{2,1,0:T(8,128)(2,1)}) %reduce-scatter.14.cloned.1.call-update) | async-done | bytes 1441808 | tf_op jit(solution)/shard_map/reduce_scatter | solution.py:213
  541.5 105.6 %reduce-scatter.12.cloned.1.call-done = bf16[2,512,704]{1,2,0:T(8,128)(2,1)} async-done(((bf16[2,2048,704]{1,2,0:T(8,128)(2,1)}), bf16[2,512,704]{1,2,0:T(8,128)(2,1)}) %reduce-scatter.12.cloned.1.call-update) | async-done | bytes 1441808 | tf_op jit(solution)/shard_map/reduce_scatter | solution.py:210
  647.1 105.6 %reduce-scatter.10.cloned.1.call-done = bf16[2,512,704]{1,2,0:T(8,128)(2,1)} async-done(((bf16[2,2048,704]{1,2,0:T(8,128)(2,1)}), bf16[2,512,704]{1,2,0:T(8,128)(2,1)}) %reduce-scatter.10.cloned.1.call-update) | async-done | bytes 1441808 | tf_op jit(solution)/shard_map/reduce_scatter | solution.py:207
  (122 shorter events, 35.2 us)
Async XLA Ops:
  7.2 46.7 %copy-start.8 = (bf16[1,128,2048]{2,1,0:T(8,128)(2,1)S(1)}, bf16[1,128,2048]{2,1,0:T(8,128)(2,1)}, u32[]{:S(2)}) copy-start(bf16[1,128,2048]{2,1,0:T(8,128)(2,1)} %param.21) | copy-start | bytes 1572868
  13.9 3.9 copy-start.15
  35.5 20.3 %copy-start.10 = (bf16[1,512,512]{1,2,0:T(8,128)(2,1)}, bf16[1,512,512]{1,2,0:T(8,128)(2,1)S(1)}, u32[]{:S(2)}) copy-start(bf16[1,512,512]{1,2,0:T(8,128)(2,1)S(1)} %all-gather) | copy-start | bytes 1572868
  37.0 18.8 %copy-start.13 = (bf16[1,128,2048]{1,2,0:T(8,128)(2,1)}, bf16[1,128,2048]{1,2,0:T(8,128)(2,1)S(1)}, u32[]{:S(2)}) copy-start(bf16[1,128,2048]{1,2,0:T(8,128)(2,1)S(1)} %copy.180) | copy-start | bytes 1572868
  55.0 1.9 copy-start.17
  55.8 2.2 copy-start.2
  56.8 1.6 copy-start.4
  58.1 6.7 copy-start.6
  58.4 6.3 copy-start
  108.8 51.2 %all-to-all-start = ((bf16[2,8,60,2048]{3,0,2,1:T(2,128)(2,1)}), bf16[2,8,60,2048]{3,0,2,1:T(2,128)(2,1)}, u32[]{:S(2)}, u32[]{:S(2)}) async-start(bf16[2,8,60,2048]{3,0,2,1:T(2,128)(2,1)} %copy.129), calls=%async_computation | async-start | bytes 7864320 | tf_op jit(solution)/shard_map/all_to_all | solution.py:172
  160.1 13.7 %slice-start = ((s8[5767168]{0:T(1024)(128)(4,1)}), s8[1572864]{0:T(1024)(128)(4,1)S(1)}, s32[]{:S(2)}) async-start(s8[5767168]{0:T(1024)(128)(4,1)} %bitcast.168), calls=%async_computation.14 | async-start | bytes 3145728
  160.1 51.0 %all-to-all-start.2 = ((bf16[2,8,60,2048]{3,0,2,1:T(2,128)(2,1)}), bf16[2,8,60,2048]{3,0,2,1:T(2,128)(2,1)}, u32[]{:S(2)}, u32[]{:S(2)}) async-start(bf16[2,8,60,2048]{3,0,2,1:T(2,128)(2,1)} %copy.135), calls=%async_computation.2 | async-start | bytes 7864320 | tf_op jit(solution)/shard_map/all_to_all | solution.py:190
  164.7 9.0 %slice-start.1 = ((s8[5767168]{0:T(1024)(128)(4,1)}), s8[4194304]{0:T(1024)(128)(4,1)S(1)}, s32[]{:S(2)}) async-start(s8[5767168]{0:T(1024)(128)(4,1)} %bitcast.168), calls=%async_computation.15 | async-start | bytes 8388608
  221.1 7.9 %copy-start.22 = (bf16[2,480,704]{1,2,0:T(8,128)(2,1)}, bf16[2,480,704]{1,2,0:T(8,128)(2,1)S(1)}, u32[]{:S(2)}) copy-start(bf16[2,480,704]{1,2,0:T(8,128)(2,1)S(1)} %get-tuple-element.54) | copy-start | bytes 4055044
  221.1 18.4 %copy-start.21 = (bf16[2,480,704]{1,2,0:T(8,128)(2,1)}, bf16[2,480,704]{1,2,0:T(8,128)(2,1)S(1)}, u32[]{:S(2)}) copy-start(bf16[2,480,704]{1,2,0:T(8,128)(2,1)S(1)} %get-tuple-element.53) | copy-start | bytes 4055044
  221.1 23.8 %copy-start.20 = (bf16[2,480,704]{1,2,0:T(8,128)(2,1)}, bf16[2,480,704]{1,2,0:T(8,128)(2,1)S(1)}, u32[]{:S(2)}) copy-start(bf16[2,480,704]{1,2,0:T(8,128)(2,1)S(1)} %get-tuple-element.52) | copy-start | bytes 4055044
  234.9 50.8 %all-to-all-start.1 = ((bf16[2,8,60,2048]{3,0,2,1:T(2,128)(2,1)}), bf16[2,8,60,2048]{3,0,2,1:T(2,128)(2,1)}, u32[]{:S(2)}, u32[]{:S(2)}) async-start(bf16[2,8,60,2048]{3,0,2,1:T(2,128)(2,1)} %bitcast.149), calls=%async_computation.1 | async-start | bytes 7864320 | tf_op jit(solution)/shard_map/all_to_all | solution.py:27
  285.7 5.0 copy-start.9
  285.7 6.2 copy-start.5
  285.7 51.0 %all-to-all-start.3 = ((bf16[2,8,60,2048]{3,0,2,1:T(2,128)(2,1)}), bf16[2,8,60,2048]{3,0,2,1:T(2,128)(2,1)}, u32[]{:S(2)}, u32[]{:S(2)}) async-start(bf16[2,8,60,2048]{3,0,2,1:T(2,128)(2,1)} %bitcast.148), calls=%async_computation.3 | async-start | bytes 7864320 | tf_op jit(solution)/shard_map/all_to_all | solution.py:27
  290.4 162.2 %reduce-scatter.8.cloned.1.call-start = ((), (), s32[]{:S(2)}) async-start(), calls=%async_computation.10 | async-start | bytes 655360 | tf_op jit(solution)/shard_map/reduce_scatter | solution.py:262
  382.1 6.1 copy-start.1
  388.9 3.1 copy-start.3
  391.4 1.6 copy-start.19
  392.0 2.1 copy-start.18
  394.1 58.5 %reduce-scatter.6.cloned.1.call-start = ((), (), s32[]{:S(2)}) async-start(), calls=%async_computation.9 | async-start | bytes 655360 | tf_op jit(solution)/shard_map/reduce_scatter | solution.py:256
  394.1 5.2 copy-start.14
  398.0 1.3 copy-start.12
  401.2 140.4 %reduce-scatter.14.cloned.1.call-start = ((), (), s32[]{:S(2)}) async-start(), calls=%async_computation.13 | async-start | bytes 7208960 | tf_op jit(solution)/shard_map/reduce_scatter | solution.py:213
  409.7 237.4 %reduce-scatter.12.cloned.1.call-start = ((), (), s32[]{:S(2)}) async-start(), calls=%async_computation.12 | async-start | bytes 7208960 | tf_op jit(solution)/shard_map/reduce_scatter | solution.py:210
  418.3 334.4 %reduce-scatter.10.cloned.1.call-start = ((), (), s32[]{:S(2)}) async-start(), calls=%async_computation.11 | async-start | bytes 7208960 | tf_op jit(solution)/shard_map/reduce_scatter | solution.py:207
  427.1 1.2 copy-start.7
  439.2 5.8 copy-start.16
  444.3 6.9 copy-start.11
Sparse Core Ops, SparseCore 0:
  394.2 20.8 reduce-scatter.7
  417.9 20.1 reduce-scatter.5
  440.9 100.5 reduce-scatter.13
  544.3 102.7 reduce-scatter.11
  649.8 102.7 reduce-scatter.9
where the time goes:
time: 766 us; the launch traced here: 759 us
  waiting for transfers between devices  429 us (56%)
  local copies, waits for them, and re-layouts  142 us (19%)
  matrix products  86.4 us (11%)
  other arithmetic  35 us (5%)
  blocking collectives  32.6 us (4%)
  starting transfers between devices  19.2 us (3%)
  between operations  14.6 us (2%)
    reduce_scatter x1, waiting for transfers between devices, on_device(): lax.psum_scatter(up_sum.astype(jnp.bfloat16), 'seq', scatter_dimension=1,...  106 us
    reduce_scatter x1, waiting for transfers between devices, on_device(): lax.psum_scatter(gate_sum.astype(jnp.bfloat16), 'seq', scatter_dimension=...  106 us
    reduce_scatter x1, waiting for transfers between devices, on_device(): lax.psum_scatter(down_sum.astype(jnp.bfloat16), 'seq', scatter_dimension=...  88.9 us
    all_to_all x2, waiting for transfers between devices, collect_rows(): lax.all_to_all(results, 'expert', split_axis=1, concat_axis=1, tiled=True)  60.5 us
    all_to_all x1, waiting for transfers between devices, on_device(): lax.all_to_all(outgoing, 'expert', split_axis=1, concat_axis=1, tiled=True)  38.2 us
    all_to_all x1, waiting for transfers between devices, on_device(): lax.all_to_all(outgoing_grad, 'expert', split_axis=1, concat_axis=1, tile...  30.3 us
    all_gather x1, blocking collectives, fold_keys(): lax.all_gather(key_rows, 'seq', axis=0, tiled=True)  16.7 us
    all_gather x1, blocking collectives, fold_keys(): lax.all_gather(value_rows, 'seq', axis=0, tiled=True)  15.9 us
  transfers between devices with their start and end apart: 9, of which 7 were waited for; matrix products, arithmetic and copies ran while one was open for 15% of the time, Pallas kernels for 0%

commit v1 on v0

v1 whole, which is shorter than its diff:
```python
import functools
import math

import jax
import jax.numpy as jnp
from jax import lax
from jax.experimental import pallas as pl
from jax.experimental.pallas import tpu as pltpu
from jax.sharding import PartitionSpec as P

DH = 128
neg_big = -1e30
norm_eps = 1e-06
BF = jnp.bfloat16
F32 = jnp.float32
GATHER_BYTES = 32 * 1024 * 1024
VMEM_LIMIT = 56 * 1024 * 1024


def dot(a, b, ca, cb):
    return lax.dot_general(a, b, (((ca,), (cb,)), ((), ())), preferred_element_type=F32)


def vm():
    return pl.BlockSpec(memory_space=pltpu.VMEM)


def heads_of(ref, first, count):
    return jnp.concatenate(
        [ref[:, (first + g) * DH : (first + g + 1) * DH] for g in range(count)], axis=0
    )


def visible_mask(tokens, group, full, seq_index):
    shape = (group, tokens, full)
    pos = lax.broadcasted_iota(jnp.int32, shape, 1) + seq_index * tokens
    key = lax.broadcasted_iota(jnp.int32, shape, 2)
    return (key <= pos).reshape(group * tokens, full)


def attend_kernel(group, residual, q, kv, att, log_total, inv_rms, normed):
    tokens = q.shape[0]
    full = kv.shape[0]
    kv_heads = kv.shape[1] // (2 * DH)
    visible = visible_mask(tokens, group, full, lax.axis_index("seq"))
    scale = 1.0 / math.sqrt(DH)
    for k in range(kv_heads):
        qh = heads_of(q, k * group, group)
        kh = kv[:, k * DH : (k + 1) * DH]
        vh = kv[:, (kv_heads + k) * DH : (kv_heads + k + 1) * DH]
        scores = jnp.where(visible, dot(qh, kh, 1, 1) * scale, neg_big)
        top = jnp.max(scores, axis=1, keepdims=True)
        weights = jnp.exp(scores - top)
        total = jnp.sum(weights, axis=1, keepdims=True)
        out = (dot(weights.astype(BF), vh, 1, 0) / total).astype(BF)
        logs = top + jnp.log(total)
        for g in range(group):
            h = k * group + g
            att[:, h * DH : (h + 1) * DH] = out[g * tokens : (g + 1) * tokens]
            log_total[:, h : h + 1] = logs[g * tokens : (g + 1) * tokens]
    hidden = residual[...].astype(F32) + att[...].astype(F32)
    inv = lax.rsqrt(jnp.mean(hidden * hidden, axis=1, keepdims=True) + norm_eps)
    inv_rms[...] = inv
    normed[...] = (hidden * inv).astype(BF)


def attend(residual, q, kv, group):
    tokens, width = q.shape
    heads = width // DH
    return pl.pallas_call(
        functools.partial(attend_kernel, group),
        out_shape=(
            jax.ShapeDtypeStruct((tokens, width), BF),
            jax.ShapeDtypeStruct((tokens, heads), F32),
            jax.ShapeDtypeStruct((tokens, 1), F32),
            jax.ShapeDtypeStruct((tokens, width), BF),
        ),
        in_specs=[vm()] * 3,
        out_specs=(vm(),) * 4,
        compiler_params=pltpu.CompilerParams(vmem_limit_bytes=VMEM_LIMIT),
        cost_estimate=pl.CostEstimate(
            flops=4 * tokens * kv.shape[0] * width,
            bytes_accessed=8 * tokens * width + 2 * kv.size,
            transcendentals=heads * tokens * kv.shape[0],
        ),
        name="attend",
    )(residual, q, kv)


def attend_back_kernel(
    group, residual, q, kv, att, log_total, inv_rms, grad_out, normed_grad, res_grad, q_grad, kv_part
):
    tokens = q.shape[0]
    full = kv.shape[0]
    kv_heads = kv.shape[1] // (2 * DH)
    scale = 1.0 / math.sqrt(DH)
    inv = inv_rms[...]
    normed = (residual[...].astype(F32) + att[...].astype(F32)) * inv
    ngrad = normed_grad[...].astype(F32)
    dot_mean = jnp.mean(ngrad * normed, axis=1, keepdims=True)
    res_grad[...] = (grad_out[...].astype(F32) + inv * (ngrad - normed * dot_mean)).astype(BF)
    visible = visible_mask(tokens, group, full, lax.axis_index("seq"))
    for k in range(kv_heads):
        qh = heads_of(q, k * group, group)
        oh = heads_of(att, k * group, group)
        gh = heads_of(res_grad, k * group, group)
        logs = jnp.concatenate(
            [log_total[:, k * group + g : k * group + g + 1] for g in range(group)], axis=0
        )
        kh = kv[:, k * DH : (k + 1) * DH]
        vh = kv[:, (kv_heads + k) * DH : (kv_heads + k + 1) * DH]
        scores = jnp.where(visible, dot(qh, kh, 1, 1) * scale, neg_big)
        probs = jnp.exp(scores - logs)
        delta = jnp.sum(gh.astype(F32) * oh.astype(F32), axis=1, keepdims=True)
        pgrad = dot(gh, vh, 1, 1)
        sgrad = (probs * (pgrad - delta)).astype(BF)
        dq = (dot(sgrad, kh, 1, 0) * scale).astype(BF)
        for g in range(group):
            h = k * group + g
            q_grad[:, h * DH : (h + 1) * DH] = dq[g * tokens : (g + 1) * tokens]
        kv_part[:, k * DH : (k + 1) * DH] = (dot(sgrad, qh, 0, 0) * scale).astype(BF)
        kv_part[:, (kv_heads + k) * DH : (kv_heads + k + 1) * DH] = dot(
            probs.astype(BF), gh, 0, 0
        ).astype(BF)


def attend_back(group, residual, q, kv, att, log_total, inv_rms, grad_out, normed_grad):
    tokens, width = q.shape
    return pl.pallas_call(
        functools.partial(attend_back_kernel, group),
        out_shape=(
            jax.ShapeDtypeStruct((tokens, width), BF),
            jax.ShapeDtypeStruct((tokens, width), BF),
            jax.ShapeDtypeStruct(kv.shape, BF),
        ),
        in_specs=[vm()] * 8,
        out_specs=(vm(),) * 3,
        compiler_params=pltpu.CompilerParams(vmem_limit_bytes=VMEM_LIMIT),
        cost_estimate=pl.CostEstimate(
            flops=10 * tokens * kv.shape[0] * width,
            bytes_accessed=14 * tokens * width + 4 * kv.size,
            transcendentals=tokens * kv.shape[0] * (width // DH),
        ),
        name="attend_back",
    )(residual, q, kv, att, log_total, inv_rms, grad_out, normed_grad)


def pick_kernel(seq_index, slot, rows, picked):
    local = slot.shape[2]
    depth = picked.shape[1]
    tokens = rows.shape[2]
    row = lax.broadcasted_iota(jnp.int32, (depth, tokens), 0)
    for e in range(local):
        chosen = (slot[0, 0, e : e + 1, :] == row).astype(F32).astype(BF)
        picked[e] = dot(chosen, rows[0, 0], 1, 0).astype(BF)


def pick_rows(gathered, slot, seq_index, first, planes, depth):
    seqs, ranks, tokens, width = gathered.shape
    local = slot.shape[2]
    count = planes * ranks

    def source(i, s):
        return (lax.rem(s[0] + first + i // ranks, seqs), lax.rem(i, ranks), 0, 0)

    return pl.pallas_call(
        pick_kernel,
        out_shape=jax.ShapeDtypeStruct((local, count * depth, width), BF),
        grid_spec=pltpu.PrefetchScalarGridSpec(
            num_scalar_prefetch=1,
            grid=(count,),
            in_specs=[
                pl.BlockSpec((1, 1, local, tokens), source),
                pl.BlockSpec((1, 1, tokens, width), source),
            ],
            out_specs=pl.BlockSpec((local, depth, width), lambda i, s: (0, i, 0)),
        ),
        compiler_params=pltpu.CompilerParams(vmem_limit_bytes=16 * 1024 * 1024),
        cost_estimate=pl.CostEstimate(
            flops=2 * local * count * depth * tokens * width,
            bytes_accessed=2 * count * (tokens + local * depth) * width,
            transcendentals=0,
        ),
        name="pick_rows",
    )(seq_index, slot, gathered)


def spread_kernel(slot, rows, out):
    ranks, local, tokens = slot.shape
    depth = rows.shape[1]
    row = lax.broadcasted_iota(jnp.int32, (depth, tokens), 0)
    total = None
    for e in range(local):
        chosen = (slot[0, e : e + 1, :] == row).astype(F32).astype(BF)
        part = dot(chosen, rows[e], 0, 0)
        total = part if total is None else total + part
    out[0] = total.astype(BF)


def spread_rows(rows, slot):
    ranks, local, tokens = slot.shape
    width = rows.shape[2]
    depth = rows.shape[1] // ranks
    return pl.pallas_call(
        spread_kernel,
        out_shape=jax.ShapeDtypeStruct((ranks, tokens, width), BF),
        grid=(ranks,),
        in_specs=[
            pl.BlockSpec((1, local, tokens), lambda i: (i, 0, 0)),
            pl.BlockSpec((local, depth, width), lambda i: (0, i, 0)),
        ],
        out_specs=pl.BlockSpec((1, tokens, width), lambda i: (i, 0, 0)),
        compiler_params=pltpu.CompilerParams(vmem_limit_bytes=16 * 1024 * 1024),
        cost_estimate=pl.CostEstimate(
            flops=2 * local * ranks * depth * tokens * width,
            bytes_accessed=2 * ranks * (tokens + local * depth) * width,
            transcendentals=0,
        ),
        name="spread_rows",
    )(slot, rows)


def hidden_units(rows, grads, mix, gate_weight, up_weight, down_weight):
    gate_pre = jnp.einsum("erd,edf->erf", rows, gate_weight, preferred_element_type=F32)
    up_pre = jnp.einsum("erd,edf->erf", rows, up_weight, preferred_element_type=F32)
    raw = jnp.einsum("erd,efd->erf", grads, down_weight, preferred_element_type=F32)
    sigmoid = jax.nn.sigmoid(gate_pre)
    silu = gate_pre * sigmoid
    act = silu * up_pre
    act_grad = raw * mix[:, :, None]
    gate_grad = (act_grad * up_pre * sigmoid * (1.0 + gate_pre * (1.0 - sigmoid))).astype(BF)
    up_grad = (act_grad * silu).astype(BF)
    mixed = (act * mix[:, :, None]).astype(BF)
    return (gate_grad, up_grad, mixed, act, raw)


def on_device(
    residual,
    queries,
    key_input,
    value_input,
    routes,
    mix_weights,
    gate_weight,
    up_weight,
    down_weight,
    grad_out,
):
    tokens = residual.shape[1]
    width = residual.shape[2]
    kv_width = key_input.shape[2]
    group = queries.shape[2] // kv_width
    local = gate_weight.shape[0]
    ranks = lax.axis_size("expert")
    seqs = lax.axis_size("seq")
    experts = local * ranks
    top_count = routes.shape[2]
    capacity = tokens * top_count * 5 // (4 * experts)
    depth = -(-capacity // 16) * 16
    both = ("seq", "expert")
    seq_index = lax.axis_index("seq")
    rank_index = lax.axis_index("expert")
    seq_array = seq_index.astype(jnp.int32).reshape(1)

    kv_mine = jnp.concatenate(
        [key_input.reshape(tokens, kv_width), value_input.reshape(tokens, kv_width)], axis=1
    )
    kv = lax.all_gather(kv_mine, "seq", axis=0, tiled=True)

    expert_ids = jnp.arange(experts, dtype=jnp.int32)
    picked = routes.reshape(tokens, top_count)
    mix_rows = mix_weights.reshape(tokens, top_count)
    hit = picked[None, :, :] == expert_ids[:, None, None]
    table = jnp.sum(jnp.where(hit, mix_rows[None], 0.0), axis=2) - (
        1.0 - jnp.sum(hit.astype(F32), axis=2)
    )
    tables = lax.all_gather(table, both, axis=0, tiled=False)
    mine = lax.dynamic_slice_in_dim(tables, rank_index * local, local, axis=1)
    routed = mine >= 0.0
    before = jnp.triu(jnp.ones((tokens, tokens), BF), 1)
    rank = jnp.einsum("bet,tu->beu", routed.astype(BF), before, preferred_element_type=F32)
    slot = jnp.where(routed, rank.astype(jnp.int32), -1)
    slot = slot.reshape(seqs, ranks, local, tokens)
    mine = mine.reshape(seqs, ranks, local, tokens)

    grad_rows = grad_out.reshape(tokens, width)
    grads_all = lax.all_gather(grad_rows, both, axis=0, tiled=True)
    grads_all = grads_all.reshape(seqs, ranks, tokens, width)

    q = queries.reshape(tokens, width)
    res = residual.reshape(tokens, width)
    att, log_total, inv_rms, normed_bf = attend(res, q, kv, group)
    grads_own = pick_rows(grads_all, slot, seq_array, 0, 1, depth)
    grads_far = pick_rows(grads_all, slot, seq_array, 1, seqs - 1, depth)
    if 2 * grads_all.size > GATHER_BYTES:
        normed_bf, grads_own, grads_far = lax.optimization_barrier(
            (normed_bf, grads_own, grads_far)
        )
    normed_all = lax.all_gather(normed_bf, both, axis=0, tiled=True)
    normed_all = normed_all.reshape(seqs, ranks, tokens, width)

    slot_turned = jnp.roll(slot, -seq_index, axis=0)
    mix_turned = jnp.roll(mine, -seq_index, axis=0)
    here = slot_turned[..., None, :] == jnp.arange(depth, dtype=jnp.int32)[:, None]
    mix_slot = jnp.sum(jnp.where(here, mix_turned[..., None, :], 0.0), axis=4)
    mix_slot = jnp.transpose(mix_slot, (2, 0, 1, 3)).reshape(local, seqs * ranks * depth)
    own = ranks * depth

    rows_own = pick_rows(normed_all, slot, seq_array, 0, 1, depth)
    rows_far = pick_rows(normed_all, slot, seq_array, 1, seqs - 1, depth)
    weights = (gate_weight, up_weight, down_weight)
    gate_own, up_own, mixed_own, act_own, raw_own = hidden_units(
        rows_own, grads_own, mix_slot[:, :own], *weights
    )
    input_grad = (
        jnp.einsum("erf,edf->erd", gate_own, gate_weight, preferred_element_type=F32)
        + jnp.einsum("erf,edf->erd", up_own, up_weight, preferred_element_type=F32)
    ).astype(BF)
    slot_own = slot_turned[0]
    input_part = spread_rows(input_grad, slot_own).reshape(ranks * tokens, width)
    normed_grad = lax.psum_scatter(input_part, "expert", scatter_dimension=0, tiled=True)

    expert_out = jnp.einsum(
        "erf,efd->erd", mixed_own, down_weight, preferred_element_type=F32
    ).astype(BF)
    out_part = spread_rows(expert_out, slot_own).reshape(ranks * tokens, width)
    routed_out = lax.psum_scatter(out_part, "expert", scatter_dimension=0, tiled=True)
    hidden = res.astype(F32) + att.astype(F32)
    layer_out = (hidden + routed_out.astype(F32)).astype(BF)

    pair_dot = jnp.sum(act_own.astype(BF).astype(F32) * raw_own, axis=2)
    pair_dot = pair_dot.reshape(local, ranks, depth)
    token_dot = jnp.sum(
        jnp.where(here[0], jnp.transpose(pair_dot, (1, 0, 2))[..., None], 0.0), axis=2
    )
    dots = lax.all_to_all(token_dot, "expert", split_axis=0, concat_axis=0, tiled=True)
    dots = dots.reshape(experts, tokens)
    mix_grad = jnp.sum(jnp.where(hit, dots[:, :, None], 0.0), axis=0)

    gate_far, up_far, mixed_far, _, _ = hidden_units(
        rows_far, grads_far, mix_slot[:, own:], *weights
    )
    share = width // seqs

    def columns(array):
        return lax.dynamic_slice_in_dim(array, seq_index * share, share, axis=2)

    def outer(a_own, a_far, b_own, b_far):
        return (
            jnp.einsum("erm,ern->emn", a_own, b_own, preferred_element_type=F32)
            + jnp.einsum("erm,ern->emn", a_far, b_far, preferred_element_type=F32)
        ).astype(BF)

    cols_own, cols_far = columns(rows_own), columns(rows_far)
    gate_share = outer(cols_own, cols_far, gate_own, gate_far)
    up_share = outer(cols_own, cols_far, up_own, up_far)
    down_share = outer(mixed_own, mixed_far, columns(grads_own), columns(grads_far))

    res_grad, q_grad, kv_part = attend_back(
        group, res, q, kv, att, log_total, inv_rms, grad_rows, normed_grad
    )
    kv_share = lax.psum_scatter(kv_part, "seq", scatter_dimension=0, tiled=True)
    return (
        layer_out.reshape(1, tokens, width),
        res_grad.reshape(1, tokens, width),
        q_grad.reshape(1, tokens, width),
        kv_share[:, :kv_width].reshape(1, tokens, kv_width),
        kv_share[:, kv_width:].reshape(1, tokens, kv_width),
        mix_grad.reshape(1, tokens, top_count),
        gate_share,
        up_share,
        down_share,
    )


def solution(mesh):
    rows = P("expert", "seq", None)
    weight = P("expert", None, None)
    return jax.shard_map(
        on_device,
        mesh=mesh,
        in_specs=(rows,) * 6 + (weight,) * 3 + (rows,),
        out_specs=(rows,) * 8 + (P("expert", None, "seq"),),
        check_vma=False,
    )
```

time: 766 us -> 474 us (0.62)
  waiting for transfers between devices: 429 us -> 193 us
  local copies, waits for them, and re-layouts: 142 us -> 30.5 us
  matrix products: 86.4 us -> 134 us
  Pallas kernels: 0 us -> 43.3 us
  other arithmetic: 35 us -> 7.95 us
  starting transfers between devices: 19.2 us -> 3.98 us
  blocking collectives: 32.6 us -> 42.3 us
    reduce_scatter x5 -> x3, waiting for transfers between devices: 300 us -> 1.55 us  [the longest x1 1.53 us: on_device(): kv_share = lax.psum_scatter(kv_part, 'seq', scatter_dimension=0, tiled=True)]
    all_gather x0 -> x3, waiting for transfers between devices: none -> 191 us  [the longest x1 92.9 us: on_device(): normed_all = lax.all_gather(normed_bf, both, axis=0, tiled=True)]
    all_to_all x4 -> x1, waiting for transfers between devices: 129 us -> 0.01 us  [on_device(): lax.all_to_all(token_dot, 'expert', split_axis=0, concat_axis=0, tiled=True)]
    dot_general x16, matrix products: 86.4 us -> 134 us  [the longest x3 32.4 us: outer(): jnp.einsum('erm,ern->emn', a_far, b_far, preferred_element_type=F32)]
    pallas_call x0 -> x8, Pallas kernels: none -> 43.3 us  [the longest x4 21.6 us: pick_rows(): pl.pallas_call(pick_kernel, out_shape=jax.ShapeDtypeStruct((local, count...]
    gather x6 -> x0, local copies, waits for them, and re-layouts: 41.1 us -> none  [the longest x2 10.8 us: on_device(): jnp.take(pair_grad, slot_pair, axis=0)]
    convert_element_type x9 -> x0, local copies, waits for them, and re-layouts: 26 us -> none  [the longest x1 8.02 us: on_device(): normed_grad = jnp.sum(jnp.take(input_back, slot_index, axis=0).reshape(to...]
    unnamed x54 -> x62, local copies, waits for them, and re-layouts: 6.83 us -> 28.6 us
  transfers between devices with their start and end apart: 9 -> 7, of which waited for: 7 -> 4; matrix products, arithmetic and copies ran while one was open for 15% -> 23% of each run, Pallas kernels for 0% -> 8%
where the time goes in v1:
time: 474 us; the launch traced here: 470 us
  waiting for transfers between devices  193 us (41%)
  matrix products  134 us (28%)
  Pallas kernels  43.3 us (9%)
  blocking collectives  42.3 us (9%)
  local copies, waits for them, and re-layouts  30.5 us (6%)
  between operations  14.8 us (3%)
  other arithmetic  7.95 us (2%)
    all_gather x1, waiting for transfers between devices, on_device(): normed_all = lax.all_gather(normed_bf, both, axis=0, tiled=True)  92.9 us
    all_gather x1, waiting for transfers between devices, on_device(): grads_all = lax.all_gather(grad_rows, both, axis=0, tiled=True)  66.5 us
    all_gather x1, blocking collectives, on_device(): tables = lax.all_gather(table, both, axis=0, tiled=False)  42.3 us
    dot_general x3, matrix products, outer(): jnp.einsum('erm,ern->emn', a_far, b_far, preferred_element_type=F32)  32.4 us
    all_gather x1, waiting for transfers between devices, on_device(): kv = lax.all_gather(kv_mine, 'seq', axis=0, tiled=True)  31.1 us
    unnamed x62, local copies, waits for them, and re-layouts  28.6 us
    dot_general x2, matrix products, hidden_units(): jnp.einsum('erd,efd->erf', grads, down_weight, preferred_element_type=F32)  23.6 us
    dot_general x2, matrix products, hidden_units(): jnp.einsum('erd,edf->erf', rows, gate_weight, preferred_element_type=F32)  23.5 us
  transfers between devices with their start and end apart: 7, of which 4 were waited for; matrix products, arithmetic and copies ran while one was open for 23% of the time, Pallas kernels for 8%

profile of v1, /device:TPU:0, one launch (start us, length us, event | category | flops | bytes accessed | tf_op | source)
XLA Modules:
  0.0 469.9 jit_solution(11704962719455921130)
XLA Ops:
  7.2 1.7 pad_maximum_fusion
  9.0 0.7 all-gather.10.cloned.1.call-update
  9.7 31.1 %all-gather.6.cloned.1.call-done.kv = bf16[512,1024]{1,0:T(8,128)(2,1)} async-done(((bf16[128,1024]{1,0:T(8,128)(2,1)}), bf16[512,1024]{1,0:T(8,128)(2,1)}) %all-gather.6.cloned.1.call-update) | async-done | bytes 1048592 | tf_op jit(solution)/shard_map/all_gather | solution.py:268
  40.9 4.6 attend.1
  45.6 0.7 copy.51
  46.3 0.7 copy.50
  47.0 42.3 %all-gather = f32[512,128]{1,0:T(8,128)S(1)} all-gather(f32[16,128]{1,0:T(8,128)S(1)} %subtract_subtract_fusion), channel_id=2, replica_groups=mesh['seq'=4,'expert'=8] {'seq','expert'}, dimensions={0}, use_global_device_ids=true | all-gather | bytes 270336 | tf_op jit(solution)/shard_map/all_gather | solution.py:277
  89.3 0.1 fusion.12
  89.6 1.0 select_reduce_fusion
  90.8 1.1 iota_compare_fusion
  92.0 66.5 %all-gather.10.cloned.1.call-done = bf16[1,4096,2048]{2,1,0:T(8,128)(2,1)} async-done(((bf16[1,128,2048]{2,1,0:T(8,128)(2,1)}), bf16[1,4096,2048]{2,1,0:T(8,128)(2,1)}) %all-gather.10.cloned.1.call-update) | async-done | bytes 16777232 | tf_op jit(solution)/shard_map/all_gather | solution.py:287
  158.5 5.8 %copy-done.1 = bf16[1,4096,2048]{2,1,0:T(8,128)(2,1)S(1)} copy-done((bf16[1,4096,2048]{2,1,0:T(8,128)(2,1)S(1)}, bf16[1,4096,2048]{2,1,0:T(8,128)(2,1)}, u32[]{:S(2)}) %copy-start.1) | copy-done | bytes 16777240
  164.3 2.8 pick_rows.5
  167.1 2.0 copy-done.7
  169.1 8.0 %pick_rows.7 = bf16[2,1536,2048]{2,1,0:T(8,128)(2,1)S(1)} custom-call(s32[1]{0:T(128)} %bitcast.8.seq_index, s32[4,8,2,128]{3,2,1,0:T(2,128)S(1)} %bitcast.76, bf16[4,8,128,2048]{3,2,1,0:T(8,128)(2,1)S(1)} %bitcast.71), custom_call_target="tpu_custom_call" | custom-call | flops 1610612736 | bytes 25165824 | tf_op jit(solution)/shard_map/pick_rows/pallas_call | solution.py:166
  177.1 4.5 copy-done.4
  181.6 92.9 %all-gather.8.cloned.1.call-done = bf16[4096,2048]{1,0:T(8,128)(2,1)} async-done(((bf16[128,2048]{1,0:T(8,128)(2,1)}), bf16[4096,2048]{1,0:T(8,128)(2,1)}) %all-gather.8.cloned.1.call-update) | async-done | bytes 16777232 | tf_op jit(solution)/shard_map/all_gather | solution.py:299
  274.5 5.8 %copy-done = bf16[4096,2048]{1,0:T(8,128)(2,1)S(1)} copy-done((bf16[4096,2048]{1,0:T(8,128)(2,1)S(1)}, bf16[4096,2048]{1,0:T(8,128)(2,1)}, u32[]{:S(2)}) %copy-start) | copy-done | bytes 16777240
  280.3 2.6 pick_rows.4
  282.9 6.8 %fusion.40 = f32[2,512,704]{1,2,0:T(8,128)S(1)} fusion(bf16[2,512,2048]{2,1,0:T(8,128)(2,1)S(1)} %pick_rows.4, bf16[2,2048,704]{1,2,0:T(8,128)(2,1)} %param.17), kind=kOutput, calls=%fused_computation.75 | convolution fusion | flops 2952790016 | bytes 12845056 | tf_op jit(solution)/shard_map/erd,edf->erf/dot_general | solution.py:225
  289.8 7.5 %fusion.39 = f32[2,512,704]{1,2,0:T(8,128)} fusion(bf16[2,512,2048]{2,1,0:T(8,128)(2,1)S(1)} %pick_rows.4, bf16[2,2048,704]{1,2,0:T(8,128)(2,1)} %param.16), kind=kOutput, calls=%fused_computation.74 | convolution fusion | flops 2952790016 | bytes 12845056 | tf_op jit(solution)/shard_map/erd,edf->erf/dot_general | solution.py:224
  297.3 7.0 %multiply_reduce_fusion = (f32[2,512]{1,0:T(2,128)}, bf16[2,512,704]{1,2,0:T(8,128)(2,1)S(1)}, bf16[2,512,704]{1,2,0:T(8,128)(2,1)S(1)}, bf16[2,512,704]{1,2,0:T(8,128)(2,1)S(1)}) fusion(f32[2,512,704]{1,2,0:T(8,128)S(1)} %fusion.40, f32[2,512,704]{1,2,0:T(8,128)} %fusion.39, f32[2,512]{1,0:T(2,128)S(1)} %slice-done.4, ...), kind=kOutput, calls=%fused_computation.16 | convolution fusion | flops 2967927808 | bytes 20062208 | tf_op jit(solution)/shard_map/erd,efd->erf/dot_general | solution.py:226
  304.3 7.3 %fusion.41 = f32[2,512,2048]{2,1,0:T(8,128)S(1)} fusion(bf16[2,512,704]{1,2,0:T(8,128)(2,1)S(1)} %get-tuple-element.44, bf16[2,2048,704]{1,2,0:T(8,128)(2,1)} %param.16), kind=kOutput, calls=%fused_computation.76 | convolution fusion | flops 2952790016 | bytes 15597568 | tf_op jit(solution)/shard_map/erf,edf->erd/dot_general | solution.py:316
  311.6 6.5 %add_convert_fusion.rows = bf16[2,512,2048]{2,1,0:T(8,128)(2,1)S(1)} fusion(f32[2,512,2048]{2,1,0:T(8,128)S(1)} %fusion.41, bf16[2,512,704]{1,2,0:T(8,128)(2,1)S(1)} %get-tuple-element.46, bf16[2,2048,704]{1,2,0:T(8,128)(2,1)} %param.17), kind=kOutput, calls=%fused_computation.5 | convolution fusion | flops 2956984320 | bytes 19791872 | tf_op jit(solution)/shard_map/erf,edf->erd/dot_general | solution.py:317
  318.2 4.1 spread_rows.3
  322.3 2.0 copy-done.3
  324.5 16.6 %fusion.42 = f32[2,1536,704]{1,2,0:T(8,128)} fusion(bf16[2,1536,2048]{2,1,0:T(8,128)(2,1)} %copy-done.4, bf16[2,704,2048]{2,1,0:T(8,128)(2,1)} %param.18), kind=kOutput, calls=%fused_computation.77 | convolution fusion | flops 8858370048 | bytes 27000832 | tf_op jit(solution)/shard_map/erd,efd->erf/dot_general | solution.py:226
  341.0 6.5 %convolution_convert_fusion.rows = bf16[2,512,2048]{2,1,0:T(8,128)(2,1)S(1)} fusion(bf16[2,512,704]{1,2,0:T(8,128)(2,1)S(1)} %get-tuple-element.45, bf16[2,704,2048]{2,1,0:T(8,128)(2,1)} %param.18), kind=kOutput, calls=%fused_computation.11 | convolution fusion | flops 2954887168 | bytes 11403264 | tf_op jit(solution)/shard_map/erf,efd->erd/dot_general | solution.py:323
  347.6 4.1 spread_rows.2
  351.7 2.0 copy-done.2
  353.6 8.1 %pick_rows.6 = bf16[2,1536,2048]{2,1,0:T(8,128)(2,1)S(1)} custom-call(s32[1]{0:T(128)} %bitcast.8.seq_index, s32[4,8,2,128]{3,2,1,0:T(2,128)S(1)} %bitcast.78, bf16[4,8,128,2048]{3,2,1,0:T(8,128)(2,1)S(1)} %bitcast.69), custom_call_target="tpu_custom_call" | custom-call | flops 1610612736 | bytes 25165824 | tf_op jit(solution)/shard_map/pick_rows/pallas_call | solution.py:166
  361.8 4.5 copy-done.5
  366.3 15.9 %fusion.44 = f32[2,1536,704]{1,2,0:T(8,128)} fusion(bf16[2,1536,2048]{2,1,0:T(8,128)(2,1)} %copy-done.5, bf16[2,2048,704]{1,2,0:T(8,128)(2,1)} %param.16), kind=kOutput, calls=%fused_computation.79 | convolution fusion | flops 8858370048 | bytes 27000832 | tf_op jit(solution)/shard_map/erd,edf->erf/dot_general | solution.py:224
  382.3 0.4 reduce-scatter.8.cloned.1.call-start
  382.7 12.2 %fusion.1 = f32[2,512,704]{1,2,0:T(8,128)} fusion(f32[2,1536,704]{1,2,0:T(8,128)} %fusion.42, f32[2,1536]{1,0:T(2,128)S(1)} %slice.29, bf16[2,1536,2048]{2,1,0:T(8,128)(2,1)} %copy-done.5, s32[]{:T(128)S(6)} %select_n.61, f32[2,1536,704]{1,2,0:T(8,128)} %fusion.44), kind=kOutput, calls=%fused_computation.6 | convolution fusion | flops 2229731328 | bytes 23343108 | tf_op jit(solution)/shard_map/erm,ern->emn/dot_general | solution.py:351
  394.9 16.0 %fusion.43 = f32[2,1536,704]{1,2,0:T(8,128)} fusion(bf16[2,1536,2048]{2,1,0:T(8,128)(2,1)} %copy-done.5, bf16[2,2048,704]{1,2,0:T(8,128)(2,1)} %param.17), kind=kOutput, calls=%fused_computation.78 | convolution fusion | flops 8858370048 | bytes 27000832 | tf_op jit(solution)/shard_map/erd,edf->erf/dot_general | solution.py:225
  411.0 9.3 %fusion.5 = f32[2,512,704]{1,2,0:T(8,128)S(1)} fusion(f32[2,1536,704]{1,2,0:T(8,128)S(1)} %bitcast.100, f32[2,1536,704]{1,2,0:T(8,128)} %fusion.43, f32[2,1536,704]{1,2,0:T(8,128)} %fusion.42, f32[2,1536]{1,0:T(2,128)S(1)} %slice.29, bf16[2,1536,2048]{2,1,0:T(8,128)(2,1)} %copy-done.5, s32[]{:T(128)S(6)} %select_n.61), kind=kOutput, calls=%fused_computation.10 | convolution fusion | flops 2238382080 | bytes 31993860 | tf_op jit(solution)/shard_map/erm,ern->emn/dot_general | solution.py:351
  420.3 8.9 %attend_back.1 = (bf16[128,2048]{1,0:T(8,128)(2,1)}, bf16[128,2048]{1,0:T(8,128)(2,1)}, bf16[512,1024]{1,0:T(8,128)(2,1)}) custom-call(bf16[128,2048]{1,0:T(8,128)(2,1)} %bitcast.80, bf16[128,2048]{1,0:T(8,128)(2,1)} %bitcast.83, bf16[512,1024]{1,0:T(8,128)(2,1)} %all-gather.6.cloned.1.call-done.kv, bf16[128,2048]{1,0:T(8,128)(2,1)} %get-tuple-element.16.att, ...), custom_call_target="tpu_custom_call" | custom-call | flops 1342177280 | bytes 5767168 | tf_op jit(solution)/shard_map/attend_back/pallas_call | solution.py:129
  429.3 10.9 %fusion.2 = f32[2,704,512]{2,1,0:T(8,128)} fusion(f32[2,1536,704]{1,2,0:T(8,128)} %fusion.43, f32[2,1536]{1,0:T(2,128)S(1)} %slice.29, bf16[2,1536,2048]{2,1,0:T(8,128)(2,1)} %copy-done.4, s32[]{:T(128)S(6)} %select_n.61, f32[2,1536,704]{1,2,0:T(8,128)} %fusion.44), kind=kOutput, calls=%fused_computation.7 | convolution fusion | flops 2229731328 | bytes 23343108 | tf_op jit(solution)/shard_map/erm,ern->emn/dot_general | solution.py:351
  440.3 1.7 select_reduce_fusion.1
  442.0 3.3 all-to-all-start
  445.4 4.8 %add_convert_fusion.2 = bf16[2,512,704]{1,2,0:T(8,128)(2,1)} fusion(f32[2,512,704]{1,2,0:T(8,128)} %fusion.1, bf16[2,512,704]{1,2,0:T(8,128)(2,1)} %copy-done.15, bf16[2,512,2048]{2,1,0:T(8,128)(2,1)} %copy-done.6, s32[]{:T(128)S(6)} %select_n.61), kind=kOutput, calls=%fused_computation.14 | convolution fusion | flops 739639296 | bytes 6815748 | tf_op jit(solution)/shard_map/erm,ern->emn/dot_general | solution.py:350
  450.2 3.4 add_convert_fusion.1
  453.5 3.3 add_convert_fusion.3
  456.9 0.6 copy.38
  457.5 2.2 fusion.16
  459.7 1.5 reduce-scatter.8.cloned.1.call-done
  461.2 1.7 slice_bitcast_fusion.1
  (84 shorter events, 0.8 us)
Async XLA Ops:
  7.2 33.7 %all-gather.6.cloned.1.call-start = ((), (), s32[]{:S(2)}) async-start(), calls=%async_computation.4 | async-start | bytes 1310720 | tf_op jit(solution)/shard_map/all_gather | solution.py:268
  8.9 149.6 %all-gather.10.cloned.1.call-start = ((), (), s32[]{:S(2)}) async-start(), calls=%async_computation.9 | async-start | bytes 17301504 | tf_op jit(solution)/shard_map/all_gather | solution.py:287
  9.7 264.8 %all-gather.8.cloned.1.call-start = ((), (), s32[]{:S(2)}) async-start(), calls=%async_computation.5 | async-start | bytes 17301504 | tf_op jit(solution)/shard_map/all_gather | solution.py:299
  45.5 374.8 %reduce-scatter.6.cloned.1.call-start = ((), (), s32[]{:S(2)}) async-start(), calls=%async_computation.7 | async-start | bytes 4718592 | tf_op jit(solution)/shard_map/reduce_scatter | solution.py:321
  46.3 43.0 %copy-start.17 = (s32[1,128,6]{1,2,0:T(8,128)}, s32[1,128,6]{1,2,0:T(8,128)S(1)}, u32[]{:S(2)}) copy-start(s32[1,128,6]{1,2,0:T(8,128)S(1)} %copy.51) | copy-start | bytes 9220
  90.8 76.3 %copy-start.16 = (f32[2,2048]{1,0:T(2,128)}, f32[2,2048]{1,0:T(2,128)S(1)}, u32[]{:S(2)}) copy-start(f32[2,2048]{1,0:T(2,128)S(1)} %reshape.109) | copy-start | bytes 49156
  158.5 5.8 %copy-start.1 = (bf16[1,4096,2048]{2,1,0:T(8,128)(2,1)S(1)}, bf16[1,4096,2048]{2,1,0:T(8,128)(2,1)}, u32[]{:S(2)}) copy-start(bf16[1,4096,2048]{2,1,0:T(8,128)(2,1)} %all-gather.10.cloned.1.call-done) | copy-start | bytes 50331652
  167.1 2.0 copy-start.7
  177.1 4.5 copy-start.4
  274.5 5.8 %copy-start = (bf16[4096,2048]{1,0:T(8,128)(2,1)S(1)}, bf16[4096,2048]{1,0:T(8,128)(2,1)}, u32[]{:S(2)}) copy-start(bf16[4096,2048]{1,0:T(8,128)(2,1)} %all-gather.8.cloned.1.call-done) | copy-start | bytes 50331652
  282.9 6.8 %copy-start.6 = (bf16[2,512,2048]{2,1,0:T(8,128)(2,1)}, bf16[2,512,2048]{2,1,0:T(8,128)(2,1)S(1)}, u32[]{:S(2)}) copy-start(bf16[2,512,2048]{2,1,0:T(8,128)(2,1)S(1)} %pick_rows.4) | copy-start | bytes 12582916
  282.9 14.4 %slice-start.5 = ((s8[5767168]{0:T(1024)(128)(4,1)}), s8[4194304]{0:T(1024)(128)(4,1)S(1)}, s32[]{:S(2)}) async-start(s8[5767168]{0:T(1024)(128)(4,1)} %bitcast.95), calls=%async_computation.15 | async-start | bytes 8388608
  289.7 7.5 %copy-start.8 = (bf16[2,512,2048]{2,1,0:T(8,128)(2,1)S(1)}, bf16[2,512,2048]{2,1,0:T(8,128)(2,1)}, u32[]{:S(2)}) copy-start(bf16[2,512,2048]{2,1,0:T(8,128)(2,1)} %copy-done.7) | copy-start | bytes 12582916
  289.8 7.5 %slice-start.4 = ((f32[2,2048]{1,0:T(2,128)}), f32[2,512]{1,0:T(2,128)S(1)}, s32[]{:S(2)}) async-start(f32[2,2048]{1,0:T(2,128)} %copy-done.16), calls=%async_computation.14 | async-start | bytes 8192 | tf_op jit(solution)/shard_map/slice | solution.py:313
  289.8 7.5 %slice-start.6 = ((s8[5767168]{0:T(1024)(128)(4,1)}), s8[1572864]{0:T(1024)(128)(4,1)S(1)}, s32[]{:S(2)}) async-start(s8[5767168]{0:T(1024)(128)(4,1)} %bitcast.95), calls=%async_computation.16 | async-start | bytes 3145728
  304.3 7.3 %copy-start.11 = (bf16[2,512,704]{1,2,0:T(8,128)(2,1)}, bf16[2,512,704]{1,2,0:T(8,128)(2,1)S(1)}, u32[]{:S(2)}) copy-start(bf16[2,512,704]{1,2,0:T(8,128)(2,1)S(1)} %get-tuple-element.44) | copy-start | bytes 4325380
  304.3 7.3 %copy-start.15 = (bf16[2,512,704]{1,2,0:T(8,128)(2,1)}, bf16[2,512,704]{1,2,0:T(8,128)(2,1)S(1)}, u32[]{:S(2)}) copy-start(bf16[2,512,704]{1,2,0:T(8,128)(2,1)S(1)} %get-tuple-element.46) | copy-start | bytes 4325380
  304.3 36.7 %copy-start.13 = (bf16[2,512,704]{1,2,0:T(8,128)(2,1)}, bf16[2,512,704]{1,2,0:T(8,128)(2,1)S(1)}, u32[]{:S(2)}) copy-start(bf16[2,512,704]{1,2,0:T(8,128)(2,1)S(1)} %get-tuple-element.45) | copy-start | bytes 4325380
  322.3 2.0 copy-start.3
  324.4 133.1 %reduce-scatter.4.cloned.1.call-start = ((), (), s32[]{:S(2)}) async-start(), calls=%async_computation.6 | async-start | bytes 4718592 | tf_op jit(solution)/shard_map/reduce_scatter | solution.py:327
  324.4 29.2 %slice-start = ((s8[16777216]{0:T(1024)(128)(4,1)}), s8[4194304]{0:T(1024)(128)(4,1)S(1)}, s32[]{:S(2)}) async-start(s8[16777216]{0:T(1024)(128)(4,1)} %bitcast.67), calls=%async_computation.10 | async-start | bytes 8388608
  324.4 29.2 %slice-start.1 = ((s8[16777216]{0:T(1024)(128)(4,1)}), s8[4194304]{0:T(1024)(128)(4,1)S(1)}, s32[]{:S(2)}) async-start(s8[16777216]{0:T(1024)(128)(4,1)} %bitcast.67), calls=%async_computation.11 | async-start | bytes 8388608
  324.4 29.2 %slice-start.2 = ((s8[16777216]{0:T(1024)(128)(4,1)}), s8[4194304]{0:T(1024)(128)(4,1)S(1)}, s32[]{:S(2)}) async-start(s8[16777216]{0:T(1024)(128)(4,1)} %bitcast.67), calls=%async_computation.12 | async-start | bytes 8388608
  341.0 12.6 %slice-start.3 = ((s8[16777216]{0:T(1024)(128)(4,1)}), s8[4194304]{0:T(1024)(128)(4,1)S(1)}, s32[]{:S(2)}) async-start(s8[16777216]{0:T(1024)(128)(4,1)} %bitcast.67), calls=%async_computation.13 | async-start | bytes 8388608
  351.6 2.0 copy-start.2
  361.8 4.5 copy-start.5
  382.3 79.0 %reduce-scatter.8.cloned.1.call-start = ((), (), s32[]{:S(2)}) async-start(), calls=%async_computation.8 | async-start | bytes 1310720 | tf_op jit(solution)/shard_map/reduce_scatter | solution.py:362
  382.7 28.3 %slice-start.7 = ((s8[8650752]{0:T(1024)(128)(4,1)}), s8[262144]{0:T(1024)(128)(4,1)S(1)}, s32[]{:S(2)}) async-start(s8[8650752]{0:T(1024)(128)(4,1)} %bitcast.99), calls=%async_computation.17 | async-start | bytes 524288
  382.7 28.3 %slice-start.8 = ((s8[8650752]{0:T(1024)(128)(4,1)}), s8[4194304]{0:T(1024)(128)(4,1)S(1)}, s32[]{:S(2)}) async-start(s8[8650752]{0:T(1024)(128)(4,1)} %bitcast.99), calls=%async_computation.18 | async-start | bytes 8388608
  394.9 16.1 %slice-start.9 = ((s8[8650752]{0:T(1024)(128)(4,1)}), s8[4194304]{0:T(1024)(128)(4,1)S(1)}, s32[]{:S(2)}) async-start(s8[8650752]{0:T(1024)(128)(4,1)} %bitcast.99), calls=%async_computation.19 | async-start | bytes 8388608
  429.2 11.0 %copy-start.19 = (f32[2,512]{1,0:T(2,128)S(1)}, f32[2,512]{1,0:T(2,128)}, u32[]{:S(2)}) copy-start(f32[2,512]{1,0:T(2,128)} %get-tuple-element.43) | copy-start | bytes 12292
  442.0 14.8 %all-to-all-start = ((f32[8,2,128]{2,1,0:T(2,128)}), f32[8,2,128]{2,1,0:T(2,128)S(1)}, u32[]{:S(2)}, u32[]{:S(2)}) async-start(f32[8,2,128]{2,1,0:T(2,128)} %select_reduce_fusion.1), calls=%async_computation.3 | async-start | bytes 16384 | tf_op jit(solution)/shard_map/all_to_all | solution.py:336
  445.4 4.8 %copy-start.9 = (f32[2,704,512]{2,1,0:T(8,128)S(1)}, f32[2,704,512]{2,1,0:T(8,128)}, u32[]{:S(2)}) copy-start(f32[2,704,512]{2,1,0:T(8,128)} %fusion.2) | copy-start | bytes 8650756
  445.4 4.8 %copy-start.14 = (bf16[2,512,704]{1,2,0:T(8,128)(2,1)S(1)}, bf16[2,512,704]{1,2,0:T(8,128)(2,1)}, u32[]{:S(2)}) copy-start(bf16[2,512,704]{1,2,0:T(8,128)(2,1)} %copy-done.13) | copy-start | bytes 4325380
  450.2 3.4 copy-start.12
  453.5 3.3 copy-start.18
  453.5 3.9 copy-start.10
Sparse Core Ops, SparseCore 0:
  10.1 30.6 all-gather.5
  43.7 114.7 all-gather.9
  161.9 112.5 all-gather.7
  324.5 49.3 reduce-scatter.5
  382.4 49.3 reduce-scatter.3
  433.9 27.2 reduce-scatter.7
